TPU v7x, 32 devices: a whole 2x2x4 slice. The times are simulated.
32 devices in a mesh: layer: 2 (over x), trow: 2 (over y), tcol: 8 (over z, core).
Axes of the slice: x: 2, y: 2, z: 4, core: 2. Of those that a mesh axis runs over, the one named last changes fastest.
Arguments:
- act_rows: bfloat16 [2, 1024, 4096], P('layer', ('trow', 'tcol')), may hold values from -6 to 6
- back_rows: bfloat16 [2, 1024, 4096], P('layer', ('trow', 'tcol')), may hold values from -6 to 6
- act_cols: bfloat16 [2, 2048, 4096], P('layer', ('tcol', 'trow')), may hold values from -6 to 6
- back_cols: bfloat16 [2, 2048, 4096], P('layer', ('tcol', 'trow')), may hold values from -6 to 6
Outputs:
- kernel: float32 [1024, 2048], P(('trow', 'layer'), 'tcol')
All inputs are finite; a program needn't handle non-finite values.
Results may differ from a plain program's by a relative error of at most 0.0003.
Values may be sent and summed in bfloat16 or wider, within the bound.
A program may use at most 64 MiB of HBM per device.

v0:
```python
import jax
import jax.numpy as jnp
from jax import lax
from jax.sharding import PartitionSpec as P


def kernel_terms(row_act, row_back, col_act, col_back):
    gram_act = jnp.einsum("lrd,lcd->lrc", row_act, col_act, preferred_element_type=jnp.float32)
    gram_back = jnp.einsum("lrd,lcd->lrc", row_back, col_back, preferred_element_type=jnp.float32)
    return jnp.sum(gram_act * gram_back, axis=0) / row_act.shape[2]


def local(act_rows, back_rows, act_cols, back_cols):
    col_act, col_back = (
        lax.all_gather(act_cols, "trow", axis=1, tiled=True),
        lax.all_gather(back_cols, "trow", axis=1, tiled=True),
    )
    piece = lax.all_gather((act_rows, back_rows), "tcol", axis=1, tiled=True)
    terms = kernel_terms(piece[0], piece[1], col_act, col_back)
    result = lax.psum_scatter(terms, "layer", scatter_dimension=0, tiled=True)
    return result


def solution(mesh):
    in_specs = (
        P("layer", ("trow", "tcol"), None),
        P("layer", ("trow", "tcol"), None),
        P("layer", ("tcol", "trow"), None),
        P("layer", ("tcol", "trow"), None),
    )
    out_specs = P(("trow", "layer"), "tcol")
    return jax.shard_map(local, mesh=mesh, in_specs=in_specs, out_specs=out_specs, check_vma=False)
```

profile of v0, /device:TPU:0, one launch (start us, length us, event | category | flops | bytes accessed | tf_op | source)
XLA Modules:
  0.0 200.2 jit_solution(6542647349577602154)
XLA Ops:
  6.5 0.0 all-gather.11.cloned.1.call-start
  6.5 0.7 all-gather.11.cloned.1.call-update
  7.3 0.0 all-gather.9.cloned.1.call-start
  7.3 0.7 all-gather.9.cloned.1.call-update
  8.0 0.0 all-gather.7.cloned.1.call-start
  8.1 0.7 all-gather.7.cloned.1.call-update
  8.7 0.0 all-gather.5.cloned.1.call-start
  8.8 0.5 all-gather.5.cloned.1.call-update
  9.3 0.0 reduce-scatter.2.cloned.1.call-start
  9.4 35.4 %all-gather.11.cloned.1.call-done = bf16[1,256,4096]{2,1,0:T(8,128)(2,1)} async-done(((bf16[1,128,4096]{2,1,0:T(8,128)(2,1)}), bf16[1,256,4096]{2,1,0:T(8,128)(2,1)}) %all-gather.11.cloned.1.call-update) | async-done | bytes 2097168 | tf_op jit(solution)/shard_map/all_gather | solution.py:16
  44.7 48.5 %all-gather.9.cloned.1.call-done = bf16[1,512,4096]{2,1,0:T(8,128)(2,1)} async-done(((bf16[1,64,4096]{2,1,0:T(8,128)(2,1)}), bf16[1,512,4096]{2,1,0:T(8,128)(2,1)}) %all-gather.9.cloned.1.call-update) | async-done | bytes 4194320 | tf_op jit(solution)/shard_map/all_gather | solution.py:18
  93.2 4.2 %fusion = f32[512,256]{1,0:T(8,128)S(1)} fusion(bf16[1,512,4096]{2,1,0:T(8,128)(2,1)} %all-gather.9.cloned.1.call-done, bf16[1,256,4096]{2,1,0:T(8,128)(2,1)} %all-gather.11.cloned.1.call-done), kind=kOutput, calls=%fused_computation | convolution fusion | flops 1073741824 | bytes 6815744 | tf_op jit(solution)/shard_map/lrd,lcd->lrc/dot_general | solution.py:9
  97.4 29.3 %all-gather.7.cloned.1.call-done = bf16[1,256,4096]{2,1,0:T(8,128)(2,1)} async-done(((bf16[1,128,4096]{2,1,0:T(8,128)(2,1)}), bf16[1,256,4096]{2,1,0:T(8,128)(2,1)}) %all-gather.7.cloned.1.call-update) | async-done | bytes 2097168 | tf_op jit(solution)/shard_map/all_gather | solution.py:15
  126.7 48.4 %all-gather.5.cloned.1.call-done = bf16[1,512,4096]{2,1,0:T(8,128)(2,1)} async-done(((bf16[1,64,4096]{2,1,0:T(8,128)(2,1)}), bf16[1,512,4096]{2,1,0:T(8,128)(2,1)}) %all-gather.5.cloned.1.call-update) | async-done | bytes 4194320 | tf_op jit(solution)/shard_map/all_gather | solution.py:18
  175.1 4.9 %fusion.11 = f32[512,256]{1,0:T(8,128)} fusion(f32[512,256]{1,0:T(8,128)S(1)} %fusion, bf16[1,256,4096]{2,1,0:T(8,128)(2,1)} %all-gather.7.cloned.1.call-done, bf16[1,512,4096]{2,1,0:T(8,128)(2,1)} %all-gather.5.cloned.1.call-done), kind=kOutput, calls=%fused_computation.7 | convolution fusion | flops 1074003968 | bytes 7340032 | tf_op jit(solution)/shard_map/lrd,lcd->lrc/dot_general | solution.py:8
  180.0 0.0 reduce-scatter.2.cloned.1.call-update
  180.0 13.6 %reduce-scatter.2.cloned.1.call-done = f32[256,256]{1,0:T(8,128)} async-done(((f32[512,256]{1,0:T(8,128)}), f32[256,256]{1,0:T(8,128)}) %reduce-scatter.2.cloned.1.call-update) | async-done | bytes 262160 | tf_op jit(solution)/shard_map/reduce_scatter | solution.py:20
Async XLA Ops:
  6.5 38.2 %all-gather.11.cloned.1.call-start = ((), (), s32[]{:S(2)}) async-start(), calls=%async_computation.4 | async-start | bytes 3145728 | tf_op jit(solution)/shard_map/all_gather | solution.py:16
  7.3 86.0 %all-gather.9.cloned.1.call-start = ((), (), s32[]{:S(2)}) async-start(), calls=%async_computation.3 | async-start | bytes 4718592 | tf_op jit(solution)/shard_map/all_gather | solution.py:18
  8.0 118.7 %all-gather.7.cloned.1.call-start = ((), (), s32[]{:S(2)}) async-start(), calls=%async_computation.2 | async-start | bytes 3145728 | tf_op jit(solution)/shard_map/all_gather | solution.py:15
  8.7 166.3 %all-gather.5.cloned.1.call-start = ((), (), s32[]{:S(2)}) async-start(), calls=%async_computation.1 | async-start | bytes 4718592 | tf_op jit(solution)/shard_map/all_gather | solution.py:18
  9.3 184.3 %reduce-scatter.2.cloned.1.call-start = ((), (), s32[]{:S(2)}) async-start(), calls=%async_computation.5 | async-start | bytes 786432 | tf_op jit(solution)/shard_map/reduce_scatter | solution.py:20
Sparse Core Ops, SparseCore 0:
  8.9 35.8 all-gather.10
  46.3 46.8 all-gather.8
  94.8 31.8 all-gather.6
  128.2 46.8 all-gather.4
  180.2 13.4 reduce-scatter.1
where the time goes:
time: 200 us
  waiting for transfers between devices  178 us (89%)
  between operations  13.1 us (7%)
  matrix products  9.1 us (5%)
    all_gather x2, waiting for transfers between devices, local(): piece = lax.all_gather((act_rows, back_rows), 'tcol', axis=1, tiled=True)  96.8 us
    all_gather x1, waiting for transfers between devices, local(): lax.all_gather(back_cols, 'trow', axis=1, tiled=True)  35.4 us
    all_gather x1, waiting for transfers between devices, local(): lax.all_gather(act_cols, 'trow', axis=1, tiled=True)  29.3 us
    reduce_scatter x1, waiting for transfers between devices, local(): result = lax.psum_scatter(terms, 'layer', scatter_dimension=0, tiled=True)  13.6 us
    dot_general x1, matrix products, kernel_terms(): jnp.einsum('lrd,lcd->lrc', row_act, col_act, preferred_element_type=jnp.f...  4.95 us
    dot_general x1, matrix products, kernel_terms(): jnp.einsum('lrd,lcd->lrc', row_back, col_back, preferred_element_type=jnp...  4.15 us
  transfers between devices with their start and end apart: 5, of which 5 were waited for; matrix products, arithmetic and copies ran while one was open for 2% of the time, Pallas kernels for 0%

commit v1 on v0

v1 whole, which is shorter than its diff:
```python
import functools

import jax
import jax.numpy as jnp
from jax import lax
from jax.experimental import pallas as pl
from jax.experimental.pallas import tpu as pltpu
from jax.sharding import PartitionSpec as P

MESH = pl.DeviceIdType.MESH
CORES = 2


def kernel(sizes, act_rows, back_rows, act_cols, back_cols, out, rows, cols, term, got,
           own_sem, row_recv, up_send, down_send, pair_send, col_send, col_recv, term_send, term_recv):
    layers, trows, tcols, pieces = sizes
    depth = tcols // CORES
    held, width = act_rows.shape[1:]
    part = held // pieces
    strip = act_cols.shape[1]
    share = tcols // layers
    lay, trow, me = lax.axis_index("layer"), lax.axis_index("trow"), lax.axis_index("tcol")
    z, core = me // CORES, me % CORES
    mate = z * CORES + 1 - core
    own_rows, own_cols = (act_rows, back_rows), (act_cols, back_cols)
    chunks = [(a, h) for h in range(pieces) for a in range(2)]

    def up_ok():
        return z + 1 < depth

    def down_ok():
        return z > 0

    barrier = pltpu.get_barrier_semaphore()

    def greet(device):
        pl.semaphore_signal(barrier, inc=1, device_id=device, device_id_type=MESH)

    for step in range(1, layers):
        greet({"layer": lax.rem(lay + step, layers)})
    for step in range(1, trows):
        greet({"trow": lax.rem(trow + step, trows)})
    greet({"tcol": mate})

    @pl.when(up_ok())
    def _():
        greet({"tcol": me + CORES})

    @pl.when(down_ok())
    def _():
        greet({"tcol": me - CORES})

    along = jnp.minimum(z, 1) + jnp.minimum(depth - 1 - z, 1)
    pl.semaphore_wait(barrier, layers + trows - 1 + along)

    def row_copy(origin, a, h, own, send, target):
        src = own_rows[a].at[0, pl.ds(h * part, part)] if own else rows.at[origin, a, pl.ds(h * part, part)]
        slot = a * pieces + h
        return pltpu.make_async_remote_copy(
            src_ref=src,
            dst_ref=rows.at[origin, a, pl.ds(h * part, part)],
            send_sem=send.at[origin, slot],
            recv_sem=row_recv.at[origin, slot],
            device_id={"tcol": target},
            device_id_type=MESH,
        )

    def col_copy(a, step):
        return pltpu.make_async_remote_copy(
            src_ref=own_cols[a].at[0],
            dst_ref=cols.at[a, pl.ds(pl.multiple_of(trow * strip, strip), strip)],
            send_sem=col_send.at[a, step],
            recv_sem=col_recv.at[a, trow],
            device_id={"trow": lax.rem(trow + step, trows)},
            device_id_type=MESH,
        )

    def col_arrival(a, source):
        span = pl.ds(pl.multiple_of(source * strip, strip), strip)
        pltpu.make_async_copy(cols.at[a, span], cols.at[a, span], col_recv.at[a, source]).wait()

    def row_arrival(origin, a, h):
        block = rows.at[origin, a, pl.ds(h * part, part)]
        pltpu.make_async_copy(block, block, row_recv.at[origin, a * pieces + h]).wait()

    def term_copy(origin):
        return pltpu.make_async_remote_copy(
            src_ref=term.at[origin],
            dst_ref=got.at[lay, lax.rem(origin, share)],
            send_sem=term_send.at[origin],
            recv_sem=term_recv.at[lay, lax.rem(origin, share)],
            device_id={"layer": origin // share},
            device_id_type=MESH,
        )

    for a, h in chunks:
        @pl.when(up_ok())
        def _():
            row_copy(me, a, h, True, up_send, me + CORES).start()

        @pl.when(down_ok())
        def _():
            row_copy(me, a, h, True, down_send, me - CORES).start()

    for a in range(2):
        for step in range(1, trows):
            col_copy(a, step).start()
    own = []
    for a in range(2):
        own.append(pltpu.make_async_copy(own_rows[a].at[0], rows.at[me, a], own_sem.at[a]))
        span = pl.ds(pl.multiple_of(trow * strip, strip), strip)
        own.append(pltpu.make_async_copy(own_cols[a].at[0], cols.at[a, span], own_sem.at[2 + a]))
    for copy in own:
        copy.start()
    for a, h in chunks:
        row_copy(me, a, h, True, pair_send, mate).start()

    def compute(origin_z, side):
        origin = origin_z * CORES + side

        @pl.when(side != core)
        def _():
            for a, h in chunks:
                row_arrival(origin, a, h)

        dims = (((1,), (1,)), ((), ()))
        gram_act = lax.dot_general(rows[origin, 0], cols[0], dims, preferred_element_type=jnp.float32)
        gram_back = lax.dot_general(rows[origin, 1], cols[1], dims, preferred_element_type=jnp.float32)
        term[origin] = gram_act * gram_back

        @pl.when(origin // share != lay)
        def _():
            term_copy(origin).start()

    ready = max(1, min(depth - 1, strip * (trows - 1) // held))
    for hop in range(1, depth):
        for a, h in chunks:
            @pl.when(z >= hop)
            def _():
                origin = me - hop * CORES
                row_arrival(origin, a, h)

                @pl.when(up_ok())
                def _():
                    row_copy(origin, a, h, False, up_send, me + CORES).start()

                row_copy(origin, a, h, False, pair_send, mate).start()

            @pl.when(z + hop < depth)
            def _():
                origin = me + hop * CORES
                row_arrival(origin, a, h)

                @pl.when(down_ok())
                def _():
                    row_copy(origin, a, h, False, down_send, me - CORES).start()

                row_copy(origin, a, h, False, pair_send, mate).start()

        if hop == ready:
            for copy in own:
                copy.wait()
            for a in range(2):
                for step in range(1, trows):
                    col_arrival(a, lax.rem(trow + step, trows))

            def first(i, carry):
                origin_z = z - ready + i // CORES

                @pl.when((origin_z >= 0) & (origin_z < depth))
                def _():
                    compute(origin_z, lax.rem(i, CORES))

                return carry

            lax.fori_loop(0, (2 * ready + 1) * CORES, first, 0)
        elif hop > ready:
            def later(i, carry):
                origin_z = z - hop + 2 * hop * (i // CORES)

                @pl.when((origin_z >= 0) & (origin_z < depth))
                def _():
                    compute(origin_z, lax.rem(i, CORES))

                return carry

            lax.fori_loop(0, 2 * CORES, later, 0)

    for b in range(share):
        total = term[lay * share + b]
        for step in range(1, layers):
            source = lax.rem(lay + step, layers)
            slot = got.at[source, b]
            pltpu.make_async_copy(slot, slot, term_recv.at[source, b]).wait()
            total = total + got[source, b]
        out[pl.ds(b * held, held), :] = total / width

    def drain(origin, carry):
        zo, side = origin // CORES, lax.rem(origin, CORES)

        @pl.when(origin // share != lay)
        def _():
            term_copy(origin).wait_send()

        @pl.when(side == core)
        def _():
            for a, h in chunks:
                @pl.when((zo <= z) & up_ok())
                def _():
                    row_copy(origin, a, h, False, up_send, me + CORES).wait_send()

                @pl.when((zo >= z) & down_ok())
                def _():
                    row_copy(origin, a, h, False, down_send, me - CORES).wait_send()

                row_copy(origin, a, h, False, pair_send, mate).wait_send()

        return carry

    lax.fori_loop(0, tcols, drain, 0)
    for a in range(2):
        for step in range(1, trows):
            col_copy(a, step).wait_send()


def local(sizes, act_rows, back_rows, act_cols, back_cols):
    layers, trows, tcols, pieces = sizes
    held, width = act_rows.shape[1:]
    strip = act_cols.shape[1]
    share = tcols // layers
    dma = pltpu.SemaphoreType.DMA
    return pl.pallas_call(
        functools.partial(kernel, sizes),
        out_shape=jax.ShapeDtypeStruct((share * held, trows * strip), jnp.float32),
        in_specs=[pl.BlockSpec(memory_space=pl.ANY)] * 4,
        out_specs=pl.BlockSpec(memory_space=pltpu.VMEM),
        scratch_shapes=[
            pltpu.VMEM((tcols, 2, held, width), act_rows.dtype),
            pltpu.VMEM((2, trows * strip, width), act_cols.dtype),
            pltpu.VMEM((tcols, held, trows * strip), jnp.float32),
            pltpu.VMEM((layers, share, held, trows * strip), jnp.float32),
            dma((4,)),
            dma((tcols, 2 * pieces)),
            dma((tcols, 2 * pieces)),
            dma((tcols, 2 * pieces)),
            dma((tcols, 2 * pieces)),
            dma((2, trows)),
            dma((2, trows)),
            dma((tcols,)),
            dma((layers, share)),
        ],
        compiler_params=pltpu.CompilerParams(
            collective_id=0, has_side_effects=True, vmem_limit_bytes=40 * 1024 * 1024
        ),
    )(act_rows, back_rows, act_cols, back_cols)


def solution(mesh):
    layers, trows, tcols = (mesh.shape[name] for name in ("layer", "trow", "tcol"))
    in_specs = (
        P("layer", ("trow", "tcol"), None),
        P("layer", ("trow", "tcol"), None),
        P("layer", ("tcol", "trow"), None),
        P("layer", ("tcol", "trow"), None),
    )
    out_specs = P(("trow", "layer"), "tcol")

    def body(act_rows, back_rows, act_cols, back_cols):
        held = act_rows.shape[1]
        pieces = 2 if held % 32 == 0 else 1
        return local((layers, trows, tcols, pieces), act_rows, back_rows, act_cols, back_cols)

    return jax.shard_map(body, mesh=mesh, in_specs=in_specs, out_specs=out_specs, check_vma=False)
```

time: 200 us -> 84.5 us (0.42)
  waiting for transfers between devices: 178 us -> 0 us
  Pallas kernels: 0 us -> 78.6 us
  between operations: 13.1 us -> 0.01 us
  matrix products: 9.1 us -> 0 us
  local copies, waits for them, and re-layouts: 0 us -> 5.24 us
    all_gather x4 -> x0, waiting for transfers between devices: 162 us -> none  [the longest x2 96.8 us: local(): piece = lax.all_gather((act_rows, back_rows), 'tcol', axis=1, tiled=True)]
    pallas_call x0 -> x1, Pallas kernels: none -> 78.6 us  [local(): pl.pallas_call(functools.partial(kernel, sizes), out_shape=jax.ShapeDtype...]
    reduce_scatter x1 -> x0, waiting for transfers between devices: 13.6 us -> none  [local(): result = lax.psum_scatter(terms, 'layer', scatter_dimension=0, tiled=True)]
    dot_general x2 -> x0, matrix products: 9.1 us -> none  [the longest x1 4.95 us: kernel_terms(): jnp.einsum('lrd,lcd->lrc', row_act, col_act, preferred_element_type=jnp.f...]
    unnamed x0 -> x9, local copies, waits for them, and re-layouts: none -> 5.24 us
    unnamed x5 -> x0, waiting for transfers between devices: 2.63 us -> none
  transfers between devices with their start and end apart: 5 -> 0, of which waited for: 5 -> 0; matrix products, arithmetic and copies ran while one was open for 2% -> 0% of each run, Pallas kernels for 0% -> 0%
where the time goes in v1:
time: 84.5 us; the launch traced here: 83.8 us
  Pallas kernels  78.6 us (93%)
  local copies, waits for them, and re-layouts  5.24 us (6%)
    pallas_call x1, Pallas kernels, local(): pl.pallas_call(functools.partial(kernel, sizes), out_shape=jax.ShapeDtype...  78.6 us
    unnamed x9, local copies, waits for them, and re-layouts  5.24 us

profile of v1, /device:TPU:0, one launch (start us, length us, event | category | flops | bytes accessed | tf_op | source)
XLA Modules:
  0.0 83.8 jit_solution(1070412895238786295)
XLA Ops:
  0.0 0.0 copy-start
  0.0 1.2 %copy-done = bf16[1,128,4096]{2,1,0:T(8,128)(2,1)S(1)} copy-done((bf16[1,128,4096]{2,1,0:T(8,128)(2,1)S(1)}, bf16[1,128,4096]{2,1,0:T(8,128)(2,1)}, u32[]{:S(2)}) %copy-start) | copy-done | bytes 1048600
  1.2 0.0 copy-start.1
  1.2 1.2 %copy-done.1 = bf16[1,128,4096]{2,1,0:T(8,128)(2,1)S(1)} copy-done((bf16[1,128,4096]{2,1,0:T(8,128)(2,1)S(1)}, bf16[1,128,4096]{2,1,0:T(8,128)(2,1)}, u32[]{:S(2)}) %copy-start.1) | copy-done | bytes 1048600
  2.5 0.0 copy-start.2
  2.5 1.0 %copy-done.2 = bf16[1,64,4096]{2,1,0:T(8,128)(2,1)S(1)} copy-done((bf16[1,64,4096]{2,1,0:T(8,128)(2,1)S(1)}, bf16[1,64,4096]{2,1,0:T(8,128)(2,1)}, u32[]{:S(2)}) %copy-start.2) | copy-done | bytes 524312
  3.5 0.0 copy-start.3
  3.5 1.0 %copy-done.3 = bf16[1,64,4096]{2,1,0:T(8,128)(2,1)S(1)} copy-done((bf16[1,64,4096]{2,1,0:T(8,128)(2,1)S(1)}, bf16[1,64,4096]{2,1,0:T(8,128)(2,1)}, u32[]{:S(2)}) %copy-start.3) | copy-done | bytes 524312
  4.5 78.6 %shard_map.46 = f32[256,256]{1,0:T(8,128)S(1)} custom-call(bf16[1,64,4096]{2,1,0:T(8,128)(2,1)S(1)} %copy-done.2, bf16[1,64,4096]{2,1,0:T(8,128)(2,1)S(1)} %copy-done.3, bf16[1,128,4096]{2,1,0:T(8,128)(2,1)S(1)} %copy-done, bf16[1,128,4096]{2,1,0:T(8,128)(2,1)S(1)} %copy-done.1), custom_call_target="tpu_custom_call" | custom-call | tf_op jit(solution)/shard_map/pallas_call | solution.py:232
  83.1 0.7 copy.6
Async XLA Ops:
  0.0 1.2 %copy-start = (bf16[1,128,4096]{2,1,0:T(8,128)(2,1)S(1)}, bf16[1,128,4096]{2,1,0:T(8,128)(2,1)}, u32[]{:S(2)}) copy-start(bf16[1,128,4096]{2,1,0:T(8,128)(2,1)} %act_cols.1) | copy-start | bytes 3145732
  1.2 1.2 %copy-start.1 = (bf16[1,128,4096]{2,1,0:T(8,128)(2,1)S(1)}, bf16[1,128,4096]{2,1,0:T(8,128)(2,1)}, u32[]{:S(2)}) copy-start(bf16[1,128,4096]{2,1,0:T(8,128)(2,1)} %back_cols.1) | copy-start | bytes 3145732
  2.5 1.0 %copy-start.2 = (bf16[1,64,4096]{2,1,0:T(8,128)(2,1)S(1)}, bf16[1,64,4096]{2,1,0:T(8,128)(2,1)}, u32[]{:S(2)}) copy-start(bf16[1,64,4096]{2,1,0:T(8,128)(2,1)} %act_rows.1) | copy-start | bytes 1572868
  3.5 1.0 %copy-start.3 = (bf16[1,64,4096]{2,1,0:T(8,128)(2,1)S(1)}, bf16[1,64,4096]{2,1,0:T(8,128)(2,1)}, u32[]{:S(2)}) copy-start(bf16[1,64,4096]{2,1,0:T(8,128)(2,1)} %back_rows.1) | copy-start | bytes 1572868

commit v2 on v0

v2 whole, which is shorter than its diff:
```python
import functools

import jax
import jax.numpy as jnp
from jax import lax
from jax.experimental import pallas as pl
from jax.experimental.pallas import tpu as pltpu
from jax.sharding import PartitionSpec as P

MESH = pl.DeviceIdType.MESH
CORES = 2
TRANS = (((1,), (1,)), ((), ()))


def kernel(sizes, act_rows, back_rows, act_cols, back_cols, out, rows, cols, far, term, got, made, given,
           own_sem, row_recv, up_send, down_send, pair_send, col_send, col_recv, far_send, far_recv,
           made_send, given_recv, term_send, term_recv):
    layers, trows, tcols, pieces, cut = sizes
    depth = tcols // CORES
    held, width = act_rows.shape[1:]
    part = held // pieces
    strip = act_cols.shape[1]
    group = tcols // layers * held
    lay, trow, me = lax.axis_index("layer"), lax.axis_index("trow"), lax.axis_index("tcol")
    z, core = me // CORES, me % CORES
    mate, other = z * CORES + 1 - core, 1 - trow
    own_rows, own_cols = (act_rows, back_rows), (act_cols, back_cols)
    chunks = [(a, h) for h in range(pieces) for a in range(2)]
    edge = (z == 0) | (z == depth - 1)
    inner = (z == 1) | (z == depth - 2)
    inwards = me + CORES - 2 * CORES * jnp.minimum(z, 1)
    outwards = me - CORES + 2 * CORES * jnp.minimum(jnp.maximum(z - 1, 0), 1)

    def up_ok(a):
        return z + 1 + a < depth

    def down_ok(a):
        return z > a

    barrier = pltpu.get_barrier_semaphore()

    def greet(device):
        pl.semaphore_signal(barrier, inc=1, device_id=device, device_id_type=MESH)

    for step in range(1, layers):
        greet({"layer": lax.rem(lay + step, layers)})
    greet({"trow": other})
    greet({"tcol": mate})

    @pl.when(up_ok(0))
    def _():
        greet({"tcol": me + CORES})

    @pl.when(down_ok(0))
    def _():
        greet({"tcol": me - CORES})

    along = jnp.minimum(z, 1) + jnp.minimum(depth - 1 - z, 1)
    pl.semaphore_wait(barrier, layers + 1 + along)

    def remote(src, dst, send, recv, device):
        return pltpu.make_async_remote_copy(
            src_ref=src, dst_ref=dst, send_sem=send, recv_sem=recv, device_id=device, device_id_type=MESH
        )

    def arrival(ref, sem):
        pltpu.make_async_copy(ref, ref, sem).wait()

    def row_block(origin, a, h):
        return rows.at[a, pl.ds(pl.multiple_of(origin * held + h * part, part), part)]

    def row_copy(origin, a, h, own, send, target):
        dst = row_block(origin, a, h)
        src = own_rows[a].at[0, pl.ds(h * part, part)] if own else dst
        slot = a * pieces + h
        return remote(src, dst, send.at[origin, slot], row_recv.at[origin, slot], {"tcol": target})

    def row_arrival(origin, a, h):
        arrival(row_block(origin, a, h), row_recv.at[origin, a * pieces + h])

    def strip_of(t):
        return pl.ds(pl.multiple_of(t * strip, strip), strip)

    def col_copy(a):
        return remote(own_cols[a].at[0], cols.at[a, strip_of(trow)], col_send.at[a], col_recv.at[a], {"trow": other})

    def col_arrival(a):
        arrival(cols.at[a, strip_of(other)], col_recv.at[a])

    lengths = (cut, strip - cut)
    granule = 16

    def span(t, p):
        return pl.ds(pl.multiple_of(t * strip + p * cut, granule), lengths[p])

    def far_own(p, send, device):
        src = back_cols.at[0, pl.ds(p * cut, lengths[p])]
        return remote(src, far.at[span(trow, p)], far_send.at[send], far_recv.at[trow, p], device)

    def far_relay(t, p, send, device):
        block = far.at[span(t, p)]
        return remote(block, block, far_send.at[send], far_recv.at[t, p], device)

    def far_arrival(t, p):
        arrival(far.at[span(t, p)], far_recv.at[t, p])

    def made_copy(d, t, p):
        return remote(made.at[d, span(t, p)], given.at[d, span(t, p)], made_send.at[d, t, p],
                      given_recv.at[d, t, p], {"tcol": outwards})

    def term_copy(d, t, p):
        return remote(term.at[d, span(t, p)], got.at[lay, span(t, p)], term_send.at[d, t, p],
                      term_recv.at[lay, t, p], {"layer": d})

    @pl.when(edge)
    def _():
        far_own(1, 2, {"trow": other}).start()
        far_own(0, 0, {"tcol": inwards}).start()

    for a, h in chunks:
        @pl.when(up_ok(a))
        def _():
            row_copy(me, a, h, True, up_send, me + CORES).start()

        @pl.when(down_ok(a))
        def _():
            row_copy(me, a, h, True, down_send, me - CORES).start()

    @pl.when(edge)
    def _():
        far_own(1, 1, {"tcol": inwards}).start()

    col_copy(0).start()
    own = []
    for a in range(2):
        block = rows.at[a, pl.ds(pl.multiple_of(me * held, held), held)]
        own.append(pltpu.make_async_copy(own_rows[a].at[0], block, own_sem.at[a]))
        own.append(pltpu.make_async_copy(own_cols[a].at[0], cols.at[a, strip_of(trow)], own_sem.at[2 + a]))
    for copy in own:
        copy.start()
    for a, h in chunks:
        if a == 0:
            row_copy(me, a, h, True, pair_send, mate).start()
        else:
            @pl.when(~edge)
            def _():
                row_copy(me, a, h, True, pair_send, mate).start()

    @pl.when(edge)
    def _():
        far_arrival(other, 1)
        far_relay(other, 1, 3, {"tcol": inwards}).start()

    @pl.when(inner)
    def _():
        far_arrival(trow, 0)
        far_relay(trow, 0, 4, {"trow": other}).start()

    @pl.when(~edge)
    def _():
        col_copy(1).start()

    for hop in range(1, depth):
        for a, h in chunks:
            takes = True if a == 0 else ~edge

            @pl.when((z >= hop) & takes)
            def _():
                origin = me - hop * CORES
                row_arrival(origin, a, h)

                @pl.when(up_ok(a))
                def _():
                    row_copy(origin, a, h, False, up_send, me + CORES).start()

                row_copy(origin, a, h, False, pair_send, mate).start()

            @pl.when((z + hop < depth) & takes)
            def _():
                origin = me + hop * CORES
                row_arrival(origin, a, h)

                @pl.when(down_ok(a))
                def _():
                    row_copy(origin, a, h, False, down_send, me - CORES).start()

                row_copy(origin, a, h, False, pair_send, mate).start()

    for copy in own:
        copy.wait()

    def from_mate(i, carry):
        origin = i * CORES + 1 - core
        for h in range(pieces):
            row_arrival(origin, 0, h)

            @pl.when(~edge)
            def _():
                row_arrival(origin, 1, h)

        return carry

    lax.fori_loop(0, depth, from_mate, 0)

    def rows_of(a, d):
        return rows[a, pl.ds(pl.multiple_of(d * group, group), group), :]

    def each_layer(body):
        def step(i, carry):
            body(lax.rem(lay + 1 + i, layers))
            return carry

        lax.fori_loop(0, layers, step, 0)

    def send_term(d, t, p):
        @pl.when(d != lay)
        def _():
            term_copy(d, t, p).start()

    def make_far(t, p):
        def body(d):
            made[d, span(t, p), :] = lax.dot_general(
                far[span(t, p), :], rows_of(1, d), TRANS, preferred_element_type=jnp.float32)
            made_copy(d, t, p).start()

        far_arrival(t, p)
        each_layer(body)

    @pl.when(inner)
    def _():
        def body(d):
            made[d, span(trow, 0), :] = lax.dot_general(
                far[span(trow, 0), :], rows_of(1, d), TRANS, preferred_element_type=jnp.float32)
            made_copy(d, trow, 0).start()

        each_layer(body)
        make_far(other, 0)
        make_far(trow, 1)

    col_arrival(0)

    def gram_act(d):
        term[d] = lax.dot_general(cols[0], rows_of(0, d), TRANS, preferred_element_type=jnp.float32)

    each_layer(gram_act)

    def gram_back(t):
        def body(d):
            strips = strip_of(t)
            term[d, strips, :] = term[d, strips, :] * lax.dot_general(
                cols[1, strips, :], rows_of(1, d), TRANS, preferred_element_type=jnp.float32)
            for p in range(2):
                send_term(d, t, p)

        each_layer(body)

    @pl.when(~edge)
    def _():
        gram_back(trow)

    @pl.when(inner)
    def _():
        make_far(other, 1)

    @pl.when(~edge)
    def _():
        col_arrival(1)
        gram_back(other)

    @pl.when(edge)
    def _():
        for t, p in ((trow, 0), (other, 0), (trow, 1), (other, 1)):
            def body(d):
                block = given.at[d, span(t, p)]
                arrival(block, given_recv.at[d, t, p])
                term[d, span(t, p), :] = term[d, span(t, p), :] * given[d, span(t, p), :]
                send_term(d, t, p)

            each_layer(body)

    for step in range(1, layers):
        source = lax.rem(lay + step, layers)
        for t in range(2):
            for p in range(2):
                arrival(got.at[source, span(t, p)], term_recv.at[source, t, p])
    total = term[lay]
    for step in range(1, layers):
        total = total + got[lax.rem(lay + step, layers)]
    out[...] = total.T / width

    def drain(i, carry):
        origin = i * CORES + core
        for a, h in chunks:
            takes = True if a == 0 else (~edge | (i == z))

            @pl.when((i <= z) & up_ok(a) & takes)
            def _():
                row_copy(origin, a, h, False, up_send, me + CORES).wait_send()

            @pl.when((i >= z) & down_ok(a) & takes)
            def _():
                row_copy(origin, a, h, False, down_send, me - CORES).wait_send()

            if a == 0:
                row_copy(origin, a, h, False, pair_send, mate).wait_send()
            else:
                @pl.when(~edge)
                def _():
                    row_copy(origin, a, h, False, pair_send, mate).wait_send()

        return carry

    lax.fori_loop(0, depth, drain, 0)
    col_copy(0).wait_send()

    @pl.when(~edge)
    def _():
        col_copy(1).wait_send()

    @pl.when(edge)
    def _():
        far_own(0, 0, {"tcol": inwards}).wait_send()
        far_own(1, 1, {"tcol": inwards}).wait_send()
        far_own(1, 2, {"trow": other}).wait_send()
        far_relay(other, 1, 3, {"tcol": inwards}).wait_send()

    @pl.when(inner)
    def _():
        far_relay(trow, 0, 4, {"trow": other}).wait_send()

    def drain_terms(d):
        for t in range(2):
            for p in range(2):
                @pl.when(d != lay)
                def _():
                    term_copy(d, t, p).wait_send()

                @pl.when(inner)
                def _():
                    made_copy(d, t, p).wait_send()

    each_layer(drain_terms)


def local(sizes, act_rows, back_rows, act_cols, back_cols):
    layers, trows, tcols, pieces, cut = sizes
    held, width = act_rows.shape[1:]
    strip = act_cols.shape[1]
    group = tcols // layers * held
    dma = pltpu.SemaphoreType.DMA
    grams = pltpu.VMEM((layers, trows * strip, group), jnp.float32)
    return pl.pallas_call(
        functools.partial(kernel, sizes),
        out_shape=jax.ShapeDtypeStruct((group, trows * strip), jnp.float32),
        in_specs=[pl.BlockSpec(memory_space=pl.ANY)] * 4,
        out_specs=pl.BlockSpec(memory_space=pltpu.VMEM),
        scratch_shapes=[
            pltpu.VMEM((2, tcols * held, width), act_rows.dtype),
            pltpu.VMEM((2, trows * strip, width), act_cols.dtype),
            pltpu.VMEM((trows * strip, width), act_cols.dtype),
            grams, grams, grams, grams,
            dma((4,)),
            dma((tcols, 2 * pieces)),
            dma((tcols, 2 * pieces)),
            dma((tcols, 2 * pieces)),
            dma((tcols, 2 * pieces)),
            dma((2,)),
            dma((2,)),
            dma((5,)),
            dma((2, 2)),
            dma((layers, 2, 2)),
            dma((layers, 2, 2)),
            dma((layers, 2, 2)),
            dma((layers, 2, 2)),
        ],
        compiler_params=pltpu.CompilerParams(
            collective_id=0, has_side_effects=True, vmem_limit_bytes=40 * 1024 * 1024
        ),
    )(act_rows, back_rows, act_cols, back_cols)


def solution(mesh):
    layers, trows, tcols = (mesh.shape[name] for name in ("layer", "trow", "tcol"))
    in_specs = (
        P("layer", ("trow", "tcol"), None),
        P("layer", ("trow", "tcol"), None),
        P("layer", ("tcol", "trow"), None),
        P("layer", ("tcol", "trow"), None),
    )
    out_specs = P(("trow", "layer"), "tcol")

    def body(act_rows, back_rows, act_cols, back_cols):
        held, strip = act_rows.shape[1], act_cols.shape[1]
        pieces = 2 if held % 32 == 0 else 1
        cut = strip // 2
        return local((layers, trows, tcols, pieces, cut), act_rows, back_rows, act_cols, back_cols)

    return jax.shard_map(body, mesh=mesh, in_specs=in_specs, out_specs=out_specs, check_vma=False)
```

time: 200 us -> 75.8 us (0.38)
  waiting for transfers between devices: 178 us -> 0 us
  Pallas kernels: 0 us -> 70.3 us
  between operations: 13.1 us -> 0.01 us
  matrix products: 9.1 us -> 0 us
  local copies, waits for them, and re-layouts: 0 us -> 5.24 us
    all_gather x4 -> x0, waiting for transfers between devices: 162 us -> none  [the longest x2 96.8 us: local(): piece = lax.all_gather((act_rows, back_rows), 'tcol', axis=1, tiled=True)]
    pallas_call x0 -> x1, Pallas kernels: none -> 70.3 us  [local(): pl.pallas_call(functools.partial(kernel, sizes), out_shape=jax.ShapeDtype...]
    reduce_scatter x1 -> x0, waiting for transfers between devices: 13.6 us -> none  [local(): result = lax.psum_scatter(terms, 'layer', scatter_dimension=0, tiled=True)]
    dot_general x2 -> x0, matrix products: 9.1 us -> none  [the longest x1 4.95 us: kernel_terms(): jnp.einsum('lrd,lcd->lrc', row_act, col_act, preferred_element_type=jnp.f...]
    unnamed x0 -> x9, local copies, waits for them, and re-layouts: none -> 5.24 us
    unnamed x5 -> x0, waiting for transfers between devices: 2.63 us -> none
  transfers between devices with their start and end apart: 5 -> 0, of which waited for: 5 -> 0; matrix products, arithmetic and copies ran while one was open for 2% -> 0% of each run, Pallas kernels for 0% -> 0%
where the time goes in v2:
time: 75.8 us; the launch traced here: 75.5 us
  Pallas kernels  70.3 us (93%)
  local copies, waits for them, and re-layouts  5.24 us (7%)
    pallas_call x1, Pallas kernels, local(): pl.pallas_call(functools.partial(kernel, sizes), out_shape=jax.ShapeDtype...  70.3 us
    unnamed x9, local copies, waits for them, and re-layouts  5.24 us

profile of v2, /device:TPU:0, one launch (start us, length us, event | category | flops | bytes accessed | tf_op | source)
XLA Modules:
  0.0 75.5 jit_solution(12887071168024153672)
XLA Ops:
  0.0 0.0 copy-start
  0.0 1.2 %copy-done = bf16[1,128,4096]{2,1,0:T(8,128)(2,1)S(1)} copy-done((bf16[1,128,4096]{2,1,0:T(8,128)(2,1)S(1)}, bf16[1,128,4096]{2,1,0:T(8,128)(2,1)}, u32[]{:S(2)}) %copy-start) | copy-done | bytes 1048600
  1.2 0.0 copy-start.1
  1.2 1.2 %copy-done.1 = bf16[1,128,4096]{2,1,0:T(8,128)(2,1)S(1)} copy-done((bf16[1,128,4096]{2,1,0:T(8,128)(2,1)S(1)}, bf16[1,128,4096]{2,1,0:T(8,128)(2,1)}, u32[]{:S(2)}) %copy-start.1) | copy-done | bytes 1048600
  2.5 0.0 copy-start.2
  2.5 1.0 %copy-done.2 = bf16[1,64,4096]{2,1,0:T(8,128)(2,1)S(1)} copy-done((bf16[1,64,4096]{2,1,0:T(8,128)(2,1)S(1)}, bf16[1,64,4096]{2,1,0:T(8,128)(2,1)}, u32[]{:S(2)}) %copy-start.2) | copy-done | bytes 524312
  3.5 0.0 copy-start.3
  3.5 1.0 %copy-done.3 = bf16[1,64,4096]{2,1,0:T(8,128)(2,1)S(1)} copy-done((bf16[1,64,4096]{2,1,0:T(8,128)(2,1)S(1)}, bf16[1,64,4096]{2,1,0:T(8,128)(2,1)}, u32[]{:S(2)}) %copy-start.3) | copy-done | bytes 524312
  4.5 70.3 %shard_map.46 = f32[256,256]{1,0:T(8,128)S(1)} custom-call(bf16[1,64,4096]{2,1,0:T(8,128)(2,1)S(1)} %copy-done.2, bf16[1,64,4096]{2,1,0:T(8,128)(2,1)S(1)} %copy-done.3, bf16[1,128,4096]{2,1,0:T(8,128)(2,1)S(1)} %copy-done, bf16[1,128,4096]{2,1,0:T(8,128)(2,1)S(1)} %copy-done.1), custom_call_target="tpu_custom_call" | custom-call | tf_op jit(solution)/shard_map/pallas_call | solution.py:352
  74.8 0.7 copy.6
Async XLA Ops:
  0.0 1.2 %copy-start = (bf16[1,128,4096]{2,1,0:T(8,128)(2,1)S(1)}, bf16[1,128,4096]{2,1,0:T(8,128)(2,1)}, u32[]{:S(2)}) copy-start(bf16[1,128,4096]{2,1,0:T(8,128)(2,1)} %act_cols.1) | copy-start | bytes 3145732
  1.2 1.2 %copy-start.1 = (bf16[1,128,4096]{2,1,0:T(8,128)(2,1)S(1)}, bf16[1,128,4096]{2,1,0:T(8,128)(2,1)}, u32[]{:S(2)}) copy-start(bf16[1,128,4096]{2,1,0:T(8,128)(2,1)} %back_cols.1) | copy-start | bytes 3145732
  2.5 1.0 %copy-start.2 = (bf16[1,64,4096]{2,1,0:T(8,128)(2,1)S(1)}, bf16[1,64,4096]{2,1,0:T(8,128)(2,1)}, u32[]{:S(2)}) copy-start(bf16[1,64,4096]{2,1,0:T(8,128)(2,1)} %act_rows.1) | copy-start | bytes 1572868
  3.5 1.0 %copy-start.3 = (bf16[1,64,4096]{2,1,0:T(8,128)(2,1)S(1)}, bf16[1,64,4096]{2,1,0:T(8,128)(2,1)}, u32[]{:S(2)}) copy-start(bf16[1,64,4096]{2,1,0:T(8,128)(2,1)} %back_rows.1) | copy-start | bytes 1572868

commit v3 on v2

--- a/solution.py
+++ b/solution.py
@@ -81,17 +81,18 @@
     def strip_of(t):
         return pl.ds(pl.multiple_of(t * strip, strip), strip)
 
-    def col_copy(a):
-        return remote(own_cols[a].at[0], cols.at[a, strip_of(trow)], col_send.at[a], col_recv.at[a], {"trow": other})
-
-    def col_arrival(a):
-        arrival(cols.at[a, strip_of(other)], col_recv.at[a])
-
     lengths = (cut, strip - cut)
     granule = 16
 
     def span(t, p):
         return pl.ds(pl.multiple_of(t * strip + p * cut, granule), lengths[p])
+
+    def col_copy(a, p):
+        src = own_cols[a].at[0, pl.ds(p * cut, lengths[p])]
+        return remote(src, cols.at[a, span(trow, p)], col_send.at[a, p], col_recv.at[a, p], {"trow": other})
+
+    def col_arrival(a, p):
+        arrival(cols.at[a, span(other, p)], col_recv.at[a, p])
 
     def far_own(p, send, device):
         src = back_cols.at[0, pl.ds(p * cut, lengths[p])]
@@ -130,7 +131,8 @@
     def _():
         far_own(1, 1, {"tcol": inwards}).start()
 
-    col_copy(0).start()
+    for p in range(2):
+        col_copy(0, p).start()
     own = []
     for a in range(2):
         block = rows.at[a, pl.ds(pl.multiple_of(me * held, held), held)]
@@ -158,7 +160,8 @@
 
     @pl.when(~edge)
     def _():
-        col_copy(1).start()
+        for p in range(2):
+            col_copy(1, p).start()
 
     for hop in range(1, depth):
         for a, h in chunks:
@@ -237,26 +240,27 @@
         make_far(other, 0)
         make_far(trow, 1)
 
-    col_arrival(0)
+    for p in range(2):
+        col_arrival(0, p)
 
     def gram_act(d):
         term[d] = lax.dot_general(cols[0], rows_of(0, d), TRANS, preferred_element_type=jnp.float32)
 
     each_layer(gram_act)
 
-    def gram_back(t):
+    def gram_back(t, p):
         def body(d):
-            strips = strip_of(t)
+            strips = span(t, p)
             term[d, strips, :] = term[d, strips, :] * lax.dot_general(
                 cols[1, strips, :], rows_of(1, d), TRANS, preferred_element_type=jnp.float32)
-            for p in range(2):
-                send_term(d, t, p)
+            send_term(d, t, p)
 
         each_layer(body)
 
     @pl.when(~edge)
     def _():
-        gram_back(trow)
+        for p in range(2):
+            gram_back(trow, p)
 
     @pl.when(inner)
     def _():
@@ -264,8 +268,9 @@
 
     @pl.when(~edge)
     def _():
-        col_arrival(1)
-        gram_back(other)
+        for p in range(2):
+            col_arrival(1, p)
+            gram_back(other, p)
 
     @pl.when(edge)
     def _():
@@ -311,11 +316,13 @@
         return carry
 
     lax.fori_loop(0, depth, drain, 0)
-    col_copy(0).wait_send()
+    for p in range(2):
+        col_copy(0, p).wait_send()
 
     @pl.when(~edge)
     def _():
-        col_copy(1).wait_send()
+        for p in range(2):
+            col_copy(1, p).wait_send()
 
     @pl.when(edge)
     def _():
@@ -364,8 +371,8 @@
             dma((tcols, 2 * pieces)),
             dma((tcols, 2 * pieces)),
             dma((tcols, 2 * pieces)),
-            dma((2,)),
-            dma((2,)),
+            dma((2, 2)),
+            dma((2, 2)),
             dma((5,)),
             dma((2, 2)),
             dma((layers, 2, 2)),
@@ -374,7 +381,7 @@
             dma((layers, 2, 2)),
         ],
         compiler_params=pltpu.CompilerParams(
-            collective_id=0, has_side_effects=True, vmem_limit_bytes=40 * 1024 * 1024
+            collective_id=0, has_side_effects=True, vmem_limit_bytes=62 * 1024 * 1024
         ),
     )(act_rows, back_rows, act_cols, back_cols)
 
@@ -392,7 +399,7 @@
     def body(act_rows, back_rows, act_cols, back_cols):
         held, strip = act_rows.shape[1], act_cols.shape[1]
         pieces = 2 if held % 32 == 0 else 1
-        cut = strip // 2
+        cut = strip * 5 // 8
         return local((layers, trows, tcols, pieces, cut), act_rows, back_rows, act_cols, back_cols)
 
     return jax.shard_map(body, mesh=mesh, in_specs=in_specs, out_specs=out_specs, check_vma=False)

time: 75.8 us -> 71.8 us (0.947)
  local copies, waits for them, and re-layouts: 5.24 us -> 1.67 us
    unnamed x9 -> x1, local copies, waits for them, and re-layouts: 5.24 us -> 1.67 us
where the time goes in v3:
time: 71.8 us; the launch traced here: 71.7 us
  Pallas kernels  70 us (97%)
  local copies, waits for them, and re-layouts  1.67 us (2%)
    pallas_call x1, Pallas kernels, local(): pl.pallas_call(functools.partial(kernel, sizes), out_shape=jax.ShapeDtype...  70 us
    unnamed x1, local copies, waits for them, and re-layouts  1.67 us

profile of v3, /device:TPU:0, one launch (start us, length us, event | category | flops | bytes accessed | tf_op | source)
XLA Modules:
  0.0 71.7 jit_solution(12396990632942039076)
XLA Ops:
  0.0 70.0 %shard_map.46 = f32[256,256]{1,0:T(8,128)} custom-call(bf16[1,64,4096]{2,1,0:T(8,128)(2,1)} %act_rows.1, bf16[1,64,4096]{2,1,0:T(8,128)(2,1)} %back_rows.1, bf16[1,128,4096]{2,1,0:T(8,128)(2,1)} %act_cols.1, bf16[1,128,4096]{2,1,0:T(8,128)(2,1)} %back_cols.1), custom_call_target="tpu_custom_call" | custom-call | tf_op jit(solution)/shard_map/pallas_call | solution.py:359
  70.0 1.7 %copy.6 = f32[256,256]{1,0:T(8,128)} copy(f32[256,256]{1,0:T(8,128)} %shard_map.46) | data formatting | bytes 524288

commit v4 on v3

--- a/solution.py
+++ b/solution.py
@@ -15,7 +15,7 @@
 def kernel(sizes, act_rows, back_rows, act_cols, back_cols, out, rows, cols, far, term, got, made, given,
            own_sem, row_recv, up_send, down_send, pair_send, col_send, col_recv, far_send, far_recv,
            made_send, given_recv, term_send, term_recv):
-    layers, trows, tcols, pieces, cut = sizes
+    layers, trows, tcols, pieces, cut, kept = sizes
     depth = tcols // CORES
     held, width = act_rows.shape[1:]
     part = held // pieces
@@ -31,12 +31,6 @@
     inwards = me + CORES - 2 * CORES * jnp.minimum(z, 1)
     outwards = me - CORES + 2 * CORES * jnp.minimum(jnp.maximum(z - 1, 0), 1)
 
-    def up_ok(a):
-        return z + 1 + a < depth
-
-    def down_ok(a):
-        return z > a
-
     barrier = pltpu.get_barrier_semaphore()
 
     def greet(device):
@@ -47,11 +41,11 @@
     greet({"trow": other})
     greet({"tcol": mate})
 
-    @pl.when(up_ok(0))
+    @pl.when(z + 1 < depth)
     def _():
         greet({"tcol": me + CORES})
 
-    @pl.when(down_ok(0))
+    @pl.when(z > 0)
     def _():
         greet({"tcol": me - CORES})
 
@@ -66,17 +60,44 @@
     def arrival(ref, sem):
         pltpu.make_async_copy(ref, ref, sem).wait()
 
-    def row_block(origin, a, h):
-        return rows.at[a, pl.ds(pl.multiple_of(origin * held + h * part, part), part)]
-
-    def row_copy(origin, a, h, own, send, target):
-        dst = row_block(origin, a, h)
-        src = own_rows[a].at[0, pl.ds(h * part, part)] if own else dst
+    def row_block(origin, a, h, narrow):
+        span = pl.ds(pl.multiple_of(origin * held + h * part, part), part)
+        return rows.at[a, span, pl.ds(0, kept)] if narrow else rows.at[a, span]
+
+    def row_copy(origin, a, h, own, send, target, narrow):
+        dst = row_block(origin, a, h, narrow)
+        src = dst
+        if own:
+            span = pl.ds(h * part, part)
+            src = own_rows[a].at[0, span, pl.ds(0, kept)] if narrow else own_rows[a].at[0, span]
         slot = a * pieces + h
         return remote(src, dst, send.at[origin, slot], row_recv.at[origin, slot], {"tcol": target})
 
+    def either(a, full, some, body):
+        if a == 0:
+            pl.when(full | some)(lambda: body(False))
+        else:
+            pl.when(full)(lambda: body(False))
+            pl.when(some)(lambda: body(True))
+
+    def go(copy, wait):
+        copy.wait_send() if wait else copy.start()
+
+    def send_up(origin, a, h, own, wait=False):
+        either(a, z + 2 < depth, z + 2 == depth,
+               lambda narrow: go(row_copy(origin, a, h, own, up_send, me + CORES, narrow), wait))
+
+    def send_down(origin, a, h, own, wait=False):
+        either(a, z > 1, z == 1,
+               lambda narrow: go(row_copy(origin, a, h, own, down_send, me - CORES, narrow), wait))
+
+    def send_pair(origin, a, h, own, wait=False):
+        either(a, ~edge, edge,
+               lambda narrow: go(row_copy(origin, a, h, own, pair_send, mate, narrow), wait))
+
     def row_arrival(origin, a, h):
-        arrival(row_block(origin, a, h), row_recv.at[origin, a * pieces + h])
+        either(a, ~edge, edge,
+               lambda narrow: arrival(row_block(origin, a, h, narrow), row_recv.at[origin, a * pieces + h]))
 
     def strip_of(t):
         return pl.ds(pl.multiple_of(t * strip, strip), strip)
@@ -87,15 +108,16 @@
     def span(t, p):
         return pl.ds(pl.multiple_of(t * strip + p * cut, granule), lengths[p])
 
-    def col_copy(a, p):
-        src = own_cols[a].at[0, pl.ds(p * cut, lengths[p])]
-        return remote(src, cols.at[a, span(trow, p)], col_send.at[a, p], col_recv.at[a, p], {"trow": other})
-
-    def col_arrival(a, p):
-        arrival(cols.at[a, span(other, p)], col_recv.at[a, p])
+    def col_copy(a, p, deep=width):
+        src = own_cols[a].at[0, pl.ds(p * cut, lengths[p]), pl.ds(0, deep)]
+        dst = cols.at[a, span(trow, p), pl.ds(0, deep)]
+        return remote(src, dst, col_send.at[a, p], col_recv.at[a, p], {"trow": other})
+
+    def col_arrival(a, p, deep=width):
+        arrival(cols.at[a, span(other, p), pl.ds(0, deep)], col_recv.at[a, p])
 
     def far_own(p, send, device):
-        src = back_cols.at[0, pl.ds(p * cut, lengths[p])]
+        src = back_cols.at[0, pl.ds(p * cut, lengths[p]), pl.ds(kept, width - kept)]
         return remote(src, far.at[span(trow, p)], far_send.at[send], far_recv.at[trow, p], device)
 
     def far_relay(t, p, send, device):
@@ -119,13 +141,8 @@
         far_own(0, 0, {"tcol": inwards}).start()
 
     for a, h in chunks:
-        @pl.when(up_ok(a))
-        def _():
-            row_copy(me, a, h, True, up_send, me + CORES).start()
-
-        @pl.when(down_ok(a))
-        def _():
-            row_copy(me, a, h, True, down_send, me - CORES).start()
+        send_up(me, a, h, True)
+        send_down(me, a, h, True)
 
     @pl.when(edge)
     def _():
@@ -141,12 +158,7 @@
     for copy in own:
         copy.start()
     for a, h in chunks:
-        if a == 0:
-            row_copy(me, a, h, True, pair_send, mate).start()
-        else:
-            @pl.when(~edge)
-            def _():
-                row_copy(me, a, h, True, pair_send, mate).start()
+        send_pair(me, a, h, True)
 
     @pl.when(edge)
     def _():
@@ -163,50 +175,41 @@
         for p in range(2):
             col_copy(1, p).start()
 
+    @pl.when(edge)
+    def _():
+        for p in range(2):
+            col_copy(1, p, kept).start()
+
     for hop in range(1, depth):
         for a, h in chunks:
-            takes = True if a == 0 else ~edge
-
-            @pl.when((z >= hop) & takes)
+            @pl.when(z >= hop)
             def _():
                 origin = me - hop * CORES
                 row_arrival(origin, a, h)
-
-                @pl.when(up_ok(a))
-                def _():
-                    row_copy(origin, a, h, False, up_send, me + CORES).start()
-
-                row_copy(origin, a, h, False, pair_send, mate).start()
-
-            @pl.when((z + hop < depth) & takes)
+                send_up(origin, a, h, False)
+                send_pair(origin, a, h, False)
+
+            @pl.when(z + hop < depth)
             def _():
                 origin = me + hop * CORES
                 row_arrival(origin, a, h)
-
-                @pl.when(down_ok(a))
-                def _():
-                    row_copy(origin, a, h, False, down_send, me - CORES).start()
-
-                row_copy(origin, a, h, False, pair_send, mate).start()
+                send_down(origin, a, h, False)
+                send_pair(origin, a, h, False)
 
     for copy in own:
         copy.wait()
 
     def from_mate(i, carry):
         origin = i * CORES + 1 - core
-        for h in range(pieces):
-            row_arrival(origin, 0, h)
-
-            @pl.when(~edge)
-            def _():
-                row_arrival(origin, 1, h)
+        for a, h in chunks:
+            row_arrival(origin, a, h)
 
         return carry
 
     lax.fori_loop(0, depth, from_mate, 0)
 
-    def rows_of(a, d):
-        return rows[a, pl.ds(pl.multiple_of(d * group, group), group), :]
+    def rows_of(a, d, start=0, stop=width):
+        return rows[a, pl.ds(pl.multiple_of(d * group, group), group), start:stop]
 
     def each_layer(body):
         def step(i, carry):
@@ -223,7 +226,7 @@
     def make_far(t, p):
         def body(d):
             made[d, span(t, p), :] = lax.dot_general(
-                far[span(t, p), :], rows_of(1, d), TRANS, preferred_element_type=jnp.float32)
+                far[span(t, p), :], rows_of(1, d, kept), TRANS, preferred_element_type=jnp.float32)
             made_copy(d, t, p).start()
 
         far_arrival(t, p)
@@ -233,7 +236,7 @@
     def _():
         def body(d):
             made[d, span(trow, 0), :] = lax.dot_general(
-                far[span(trow, 0), :], rows_of(1, d), TRANS, preferred_element_type=jnp.float32)
+                far[span(trow, 0), :], rows_of(1, d, kept), TRANS, preferred_element_type=jnp.float32)
             made_copy(d, trow, 0).start()
 
         each_layer(body)
@@ -274,11 +277,20 @@
 
     @pl.when(edge)
     def _():
+        for p in range(2):
+            col_arrival(1, p, kept)
+
+        def body(d):
+            made[d] = lax.dot_general(
+                cols[1, :, :kept], rows_of(1, d, 0, kept), TRANS, preferred_element_type=jnp.float32)
+
+        each_layer(body)
         for t, p in ((trow, 0), (other, 0), (trow, 1), (other, 1)):
             def body(d):
                 block = given.at[d, span(t, p)]
                 arrival(block, given_recv.at[d, t, p])
-                term[d, span(t, p), :] = term[d, span(t, p), :] * given[d, span(t, p), :]
+                gram = made[d, span(t, p), :] + given[d, span(t, p), :]
+                term[d, span(t, p), :] = term[d, span(t, p), :] * gram
                 send_term(d, t, p)
 
             each_layer(body)
@@ -296,22 +308,9 @@
     def drain(i, carry):
         origin = i * CORES + core
         for a, h in chunks:
-            takes = True if a == 0 else (~edge | (i == z))
-
-            @pl.when((i <= z) & up_ok(a) & takes)
-            def _():
-                row_copy(origin, a, h, False, up_send, me + CORES).wait_send()
-
-            @pl.when((i >= z) & down_ok(a) & takes)
-            def _():
-                row_copy(origin, a, h, False, down_send, me - CORES).wait_send()
-
-            if a == 0:
-                row_copy(origin, a, h, False, pair_send, mate).wait_send()
-            else:
-                @pl.when(~edge)
-                def _():
-                    row_copy(origin, a, h, False, pair_send, mate).wait_send()
+            pl.when(i <= z)(lambda: send_up(origin, a, h, False, True))
+            pl.when(i >= z)(lambda: send_down(origin, a, h, False, True))
+            send_pair(origin, a, h, False, True)
 
         return carry
 
@@ -323,6 +322,11 @@
     def _():
         for p in range(2):
             col_copy(1, p).wait_send()
+
+    @pl.when(edge)
+    def _():
+        for p in range(2):
+            col_copy(1, p, kept).wait_send()
 
     @pl.when(edge)
     def _():
@@ -350,7 +354,7 @@
 
 
 def local(sizes, act_rows, back_rows, act_cols, back_cols):
-    layers, trows, tcols, pieces, cut = sizes
+    layers, trows, tcols, pieces, cut, kept = sizes
     held, width = act_rows.shape[1:]
     strip = act_cols.shape[1]
     group = tcols // layers * held
@@ -364,7 +368,7 @@
         scratch_shapes=[
             pltpu.VMEM((2, tcols * held, width), act_rows.dtype),
             pltpu.VMEM((2, trows * strip, width), act_cols.dtype),
-            pltpu.VMEM((trows * strip, width), act_cols.dtype),
+            pltpu.VMEM((trows * strip, width - kept), act_cols.dtype),
             grams, grams, grams, grams,
             dma((4,)),
             dma((tcols, 2 * pieces)),
@@ -400,6 +404,7 @@
         held, strip = act_rows.shape[1], act_cols.shape[1]
         pieces = 2 if held % 32 == 0 else 1
         cut = strip * 5 // 8
-        return local((layers, trows, tcols, pieces, cut), act_rows, back_rows, act_cols, back_cols)
+        kept = act_rows.shape[2] // 4
+        return local((layers, trows, tcols, pieces, cut, kept), act_rows, back_rows, act_cols, back_cols)
 
     return jax.shard_map(body, mesh=mesh, in_specs=in_specs, out_specs=out_specs, check_vma=False)

time: 71.8 us -> 71.5 us (level)
  no operation moved by 1% of the time
where the time goes in v4:
time: 71.5 us; the launch traced here: 71.4 us
  Pallas kernels  69.7 us (97%)
  local copies, waits for them, and re-layouts  1.67 us (2%)
    pallas_call x1, Pallas kernels, local(): pl.pallas_call(functools.partial(kernel, sizes), out_shape=jax.ShapeDtype...  69.7 us
    unnamed x1, local copies, waits for them, and re-layouts  1.67 us

profile of v4, /device:TPU:0, one launch (start us, length us, event | category | flops | bytes accessed | tf_op | source)
XLA Modules:
  0.0 71.4 jit_solution(5053210552555320995)
XLA Ops:
  0.0 69.7 %shard_map.46 = f32[256,256]{1,0:T(8,128)} custom-call(bf16[1,64,4096]{2,1,0:T(8,128)(2,1)} %act_rows.1, bf16[1,64,4096]{2,1,0:T(8,128)(2,1)} %back_rows.1, bf16[1,128,4096]{2,1,0:T(8,128)(2,1)} %act_cols.1, bf16[1,128,4096]{2,1,0:T(8,128)(2,1)} %back_cols.1), custom_call_target="tpu_custom_call" | custom-call | tf_op jit(solution)/shard_map/pallas_call | solution.py:363
  69.7 1.7 %copy.6 = f32[256,256]{1,0:T(8,128)} copy(f32[256,256]{1,0:T(8,128)} %shard_map.46) | data formatting | bytes 524288
